TPU v7x, 256 devices: a whole 4x4x8 slice. The times are simulated.
256 devices in a mesh: blk: 32 (over y_lo, z, core), uly: 8 (over y_hi, x).
Axes of the slice: x: 4, y: 4 (y_hi: 2, y_lo: 2; y = y_hi * 2 + y_lo), z: 8, core: 2. Of those that a mesh axis runs over, the one named last changes fastest.
Arguments:
- tokens: bfloat16 [32768, 5120], P(('blk', 'uly')), may hold values from -6 to 6
- query_base: bfloat16 [32768, 5120], P(('blk', 'uly')), may hold values from -9 to 9
- key_base: bfloat16 [32768, 5120], P(('blk', 'uly')), may hold values from -9 to 9
- value_base: bfloat16 [32768, 5120], P(('blk', 'uly')), may hold values from -6 to 6
- out_grad: bfloat16 [32768, 5120], P(('blk', 'uly')), may hold values from -0.059814453 to 0.059814453
- down_q: bfloat16 [5120, 64], replicated, may hold values from -0.078125 to 0.078125
- up_q: bfloat16 [64, 5120], replicated, may hold values from -0.75 to 0.75
- down_v: bfloat16 [5120, 64], replicated, may hold values from -0.078125 to 0.078125
- up_v: bfloat16 [64, 5120], replicated, may hold values from -0.75 to 0.75
Outputs:
- attended: bfloat16 [32768, 5120], P(('blk', 'uly'))
- grad_down_q: bfloat16 [5120, 64], replicated
- grad_up_q: bfloat16 [64, 5120], P(None, 'uly')
- grad_down_v: bfloat16 [5120, 64], replicated
- grad_up_v: bfloat16 [64, 5120], P(None, 'uly')
All inputs are finite; a program needn't handle non-finite values.
Results may differ from a plain program's by a relative error of at most 0.025.
Values may be sent and summed in bfloat16 or wider, within the bound.
No kernel may reach another device: no remote copies, remote signals or barrier semaphores. Data moves between devices by JAX's collectives and lax.ppermute only.
A program may use at most 128 MiB of HBM per device.

v0:
```python
import jax
import jax.numpy as jnp
from jax import lax
from jax.sharding import PartitionSpec as P

HEAD = 128


def passed_along(block, axis, distance):
    devices = range(lax.axis_size(axis))
    route = [(i - distance, i) for i in devices if i - distance in devices]
    return lax.ppermute(block, axis, route)


def inner(left, right):
    return lax.dot_general(
        left, right, (((0,), (0,)), ((), ())), preferred_element_type=jnp.float32
    )


def head_pass(query, keys, values, upstream, usable, scale):
    scores = jnp.dot(query, keys.T, preferred_element_type=jnp.float32) * scale
    scores = jnp.where(usable[None, :], scores, -jnp.inf)
    top = jnp.max(scores, axis=1, keepdims=True)
    total = jnp.sum(jnp.exp(scores - top), axis=1, keepdims=True)
    probs = jnp.exp(scores - top - jnp.log(total)).astype(jnp.bfloat16)
    attended = jnp.dot(probs, values, preferred_element_type=jnp.float32).astype(jnp.bfloat16)
    delta = jnp.sum(
        upstream.astype(jnp.float32) * attended.astype(jnp.float32), axis=1, keepdims=True
    )
    prob_grad = jnp.dot(upstream, values.T, preferred_element_type=jnp.float32)
    score_grad = (probs.astype(jnp.float32) * (prob_grad - delta)).astype(jnp.bfloat16)
    query_grad = (jnp.dot(score_grad, keys, preferred_element_type=jnp.float32) * scale).astype(
        jnp.bfloat16
    )
    value_terms = jnp.dot(probs.T, upstream, preferred_element_type=jnp.float32)
    return (attended, query_grad, value_terms)


def per_device(tokens, query_base, key_base, value_base, out_grad, down_q, up_q, down_v, up_v):
    low_q = jnp.dot(tokens, down_q, preferred_element_type=jnp.float32).astype(jnp.bfloat16)
    low_v = jnp.dot(tokens, down_v, preferred_element_type=jnp.float32).astype(jnp.bfloat16)
    query = (
        query_base.astype(jnp.float32) + jnp.dot(low_q, up_q, preferred_element_type=jnp.float32)
    ).astype(jnp.bfloat16)
    value = (
        value_base.astype(jnp.float32) + jnp.dot(low_v, up_v, preferred_element_type=jnp.float32)
    ).astype(jnp.bfloat16)
    query_h, keys_h, values_h, upstream_h = (
        lax.all_to_all(query, "uly", split_axis=1, concat_axis=0, tiled=True),
        lax.all_to_all(key_base, "uly", split_axis=1, concat_axis=0, tiled=True),
        lax.all_to_all(value, "uly", split_axis=1, concat_axis=0, tiled=True),
        lax.all_to_all(out_grad, "uly", split_axis=1, concat_axis=0, tiled=True),
    )
    rows = query_h.shape[0]
    width = query_h.shape[1]
    heads_here = width // HEAD
    scale = HEAD ** (-0.5)
    earlier = passed_along(jnp.stack([keys_h, values_h]), "blk", 1)
    keys_all = jnp.concatenate([earlier[0], keys_h], 0)
    values_all = jnp.concatenate([earlier[1], values_h], 0)
    column = jnp.arange(2 * rows)
    usable = jnp.logical_or(column >= rows, lax.axis_index("blk") > 0)

    def per_head(index, carry):
        attended, query_grad, own_terms, prior_terms = carry
        start = index * HEAD
        result = head_pass(
            lax.dynamic_slice_in_dim(query_h, start, HEAD, 1),
            lax.dynamic_slice_in_dim(keys_all, start, HEAD, 1),
            lax.dynamic_slice_in_dim(values_all, start, HEAD, 1),
            lax.dynamic_slice_in_dim(upstream_h, start, HEAD, 1),
            usable,
            scale,
        )
        attended = lax.dynamic_update_slice_in_dim(attended, result[0], start, 1)
        query_grad = lax.dynamic_update_slice_in_dim(query_grad, result[1], start, 1)
        prior_terms = lax.dynamic_update_slice_in_dim(prior_terms, result[2][:rows], start, 1)
        own_terms = lax.dynamic_update_slice_in_dim(own_terms, result[2][rows:], start, 1)
        return (attended, query_grad, own_terms, prior_terms)

    empty_half = jnp.zeros((rows, width), jnp.bfloat16)
    empty_full = jnp.zeros((rows, width), jnp.float32)
    attended_h, query_grad_h, own_terms, prior_terms = lax.fori_loop(
        0, heads_here, per_head, (empty_half, empty_half, empty_full, empty_full)
    )
    returned = passed_along(prior_terms, "blk", -1)
    value_grad_h = (own_terms + returned).astype(jnp.bfloat16)
    rank = down_q.shape[1]
    first_col = lax.axis_index("uly") * width
    attended, query_grad, value_grad = (
        lax.all_to_all(attended_h, "uly", split_axis=0, concat_axis=1, tiled=True),
        lax.all_to_all(query_grad_h, "uly", split_axis=0, concat_axis=1, tiled=True),
        lax.all_to_all(value_grad_h, "uly", split_axis=0, concat_axis=1, tiled=True),
    )
    lowrank = jnp.concatenate(
        [
            jnp.dot(query_grad, up_q.T, preferred_element_type=jnp.float32),
            jnp.dot(value_grad, up_v.T, preferred_element_type=jnp.float32),
        ],
        1,
    ).astype(jnp.bfloat16)
    down_terms = inner(tokens, lowrank)
    up_q_terms = inner(low_q, query_grad)
    up_v_terms = inner(low_v, value_grad)
    down_total, up_q_total, up_v_total = lax.psum(
        (down_terms, up_q_terms, up_v_terms), ("blk", "uly")
    )
    up_q_part = lax.dynamic_slice_in_dim(up_q_total, first_col, width, 1)
    up_v_part = lax.dynamic_slice_in_dim(up_v_total, first_col, width, 1)
    return (
        attended,
        down_total[:, :rank].astype(jnp.bfloat16),
        up_q_part.astype(jnp.bfloat16),
        down_total[:, rank:].astype(jnp.bfloat16),
        up_v_part.astype(jnp.bfloat16),
    )


def solution(mesh):
    return jax.shard_map(
        per_device,
        mesh=mesh,
        in_specs=(
            P(("blk", "uly"), None),
            P(("blk", "uly"), None),
            P(("blk", "uly"), None),
            P(("blk", "uly"), None),
            P(("blk", "uly"), None),
            P(),
            P(),
            P(),
            P(),
        ),
        out_specs=(P(("blk", "uly"), None), P(), P(None, "uly"), P(), P(None, "uly")),
        check_vma=False,
    )
```

profile of v0, /device:TPU:7, one launch (start us, length us, event | category | flops | bytes accessed | tf_op | source)
XLA Modules:
  0.0 464.2 jit_solution(9758977872020225476)
XLA Ops:
  0.7 1.3 copy-done
  2.0 1.7 convolution_convert_fusion.3
  3.6 1.6 fusion.20
  6.5 6.8 %all-to-all-start.2 = ((bf16[128,8,640]{2,0,1:T(8,128)(2,1)}), bf16[128,8,640]{2,0,1:T(8,128)(2,1)S(1)}, u32[]{:S(2)}, u32[]{:S(2)}) async-start(bf16[128,8,640]{2,0,1:T(8,128)(2,1)} %bitcast.90), calls=%async_computation.2 | async-start | bytes 2621440 | tf_op jit(solution)/shard_map/all_to_all | solution.py:52
  13.3 2.5 copy.67
  15.8 15.6 %all-to-all-done.2 = bf16[128,8,640]{2,0,1:T(8,128)(2,1)S(1)} async-done(((bf16[128,8,640]{2,0,1:T(8,128)(2,1)}), bf16[128,8,640]{2,0,1:T(8,128)(2,1)S(1)}, u32[]{:S(2)}, u32[]{:S(2)}) %all-to-all-start.2) | async-done | bytes 1310752 | tf_op jit(solution)/shard_map/all_to_all | solution.py:52
  31.4 22.6 %all_to_all.133 = bf16[128,8,640]{2,0,1:T(8,128)(2,1)S(1)} all-to-all(bf16[128,8,640]{2,0,1:T(8,128)(2,1)} %bitcast.91), channel_id=1, replica_groups=mesh['blk'=32,'uly'=8] {'uly'}, dimensions={1} | all-to-all | bytes 2621440 | tf_op jit(solution)/shard_map/all_to_all | solution.py:51
  53.9 1.9 pad_maximum_fusion
  55.8 5.6 %collective-permute-start = (bf16[2,1024,640]{2,1,0:T(8,128)(2,1)}, bf16[2,1024,640]{2,1,0:T(8,128)(2,1)}, u32[]{:S(2)}, u32[]{:S(2)}) collective-permute-start(bf16[2,1024,640]{2,1,0:T(8,128)(2,1)} %pad_maximum_fusion), channel_id=1, source_target_pairs={{0,8},{8,16},{16,24},{24,32},{32,40},{40,48},{48,56},{56,64},{64,7... | collective-permute-start | bytes 7864328 | tf_op jit(solution)/shard_map/ppermute | solution.py:12
  61.5 2.5 copy.48
  64.0 6.0 %all-to-all-start.3 = ((bf16[128,8,640]{0,2,1:T(8,128)(2,1)}), bf16[128,8,640]{0,2,1:T(8,128)(2,1)}, u32[]{:S(2)}, u32[]{:S(2)}) async-start(bf16[128,8,640]{0,2,1:T(8,128)(2,1)} %bitcast.89), calls=%async_computation.3 | async-start | bytes 2621440 | tf_op jit(solution)/shard_map/all_to_all | solution.py:53
  70.0 1.8 convolution_convert_fusion.4
  73.5 34.2 %all-to-all-done.3 = bf16[128,8,640]{0,2,1:T(8,128)(2,1)} async-done(((bf16[128,8,640]{0,2,1:T(8,128)(2,1)}), bf16[128,8,640]{0,2,1:T(8,128)(2,1)}, u32[]{:S(2)}, u32[]{:S(2)}) %all-to-all-start.3) | async-done | bytes 1310752 | tf_op jit(solution)/shard_map/all_to_all | solution.py:53
  107.7 5.8 %all-to-all-start = ((bf16[128,8,640]{2,0,1:T(8,128)(2,1)}), bf16[128,8,640]{2,0,1:T(8,128)(2,1)}, u32[]{:S(2)}, u32[]{:S(2)}) async-start(bf16[128,8,640]{2,0,1:T(8,128)(2,1)} %bitcast.86), calls=%async_computation | async-start | bytes 2621440 | tf_op jit(solution)/shard_map/all_to_all | solution.py:50
  113.5 2.4 copy.49
  116.0 2.0 slice_bitcast_fusion
  118.1 6.8 %pad_maximum_fusion.1 = (bf16[2048,640]{1,0:T(8,128)(2,1)}, bf16[2048,640]{1,0:T(8,128)(2,1)}) fusion(bf16[1024,640]{1,0:T(8,128)(2,1)S(1)} %bitcast.77, bf16[1024,640]{1,0:T(8,128)(2,1)S(1)} %get-tuple-element.289, bf16[1024,640]{1,0:T(8,128)(2,1)S(1)} %bitcast.75, bf16[1024,640]{1,0:T(8,128)(2,1)S(1)} %get-tuple-element.288), kind=kLoop, calls=%fused_computation.33 | loop fusion | flops 10485760 | bytes 10485760 | tf_op jit(solution)/shard_map/concatenate | solution.py:60
  124.8 6.9 %all-to-all-done = bf16[128,8,640]{2,0,1:T(8,128)(2,1)} async-done(((bf16[128,8,640]{2,0,1:T(8,128)(2,1)}), bf16[128,8,640]{2,0,1:T(8,128)(2,1)}, u32[]{:S(2)}, u32[]{:S(2)}) %all-to-all-start) | async-done | bytes 1310752 | tf_op jit(solution)/shard_map/all_to_all | solution.py:50
  131.7 1.6 broadcast_in_dim.43
  133.3 1.7 broadcast_in_dim.43.clone
  136.3 103.0 %while.20 = (s32[]{:T(128)}, bf16[1024,640]{1,0:T(8,128)(2,1)S(1)}, bf16[1024,640]{1,0:T(8,128)(2,1)}, f32[1024,640]{1,0:T(8,128)}, f32[1024,640]{1,0:T(8,128)},...) while((s32[]{:T(128)}, bf16[1024,640]{1,0:T(8,128)(2,1)S(1)}, ...), condition=%wide.region_4.5_spmd.clone, body=%wide.region_0.4_spmd.clone.sunk | while | flops 2718827520 | bytes 67680992 | solution.py:84
  136.3 2.6 fusion.67
  138.9 2.2 exponential_reduce_fusion.2
  141.1 2.3 exponential_convert_fusion.2
  144.6 1.3 fusion.69
  147.2 3.8 multiply_reduce_fusion.2
  151.0 5.6 %fusion.68 = bf16[1024,640]{1,0:T(8,128)(2,1)} fusion(bf16[1024,640]{1,0:T(8,128)(2,1)} %get-tuple-element.383, s32[]{:T(128)S(6)} %select_n.43, bf16[1024,2048]{1,0:T(8,128)(2,1)} %copy-done.1, bf16[1024,128]{1,0:T(8,128)(2,1)S(1)} %constant_dynamic-slice_fusion.2, f32[1024]{0:T(1024)S(1)} %get-tuple-element.364, ...), kind=kOutput, calls=%fused_computation.10.clone.1 | convolution fusion | flops 1082392576 | bytes 5772800 | tf_op jit(solution)/shard_map/while/body/eval_jaxpr/dot_general | solution.py:33
  157.0 2.6 fusion.67
  159.5 2.2 exponential_reduce_fusion.2
  161.8 2.3 exponential_convert_fusion.2
  167.8 3.8 multiply_reduce_fusion.2
  171.6 5.6 %fusion.68 = bf16[1024,640]{1,0:T(8,128)(2,1)} fusion(bf16[1024,640]{1,0:T(8,128)(2,1)} %get-tuple-element.383, s32[]{:T(128)S(6)} %select_n.43, bf16[1024,2048]{1,0:T(8,128)(2,1)} %copy-done.1, bf16[1024,128]{1,0:T(8,128)(2,1)S(1)} %constant_dynamic-slice_fusion.2, f32[1024]{0:T(1024)S(1)} %get-tuple-element.364, ...), kind=kOutput, calls=%fused_computation.10.clone.1 | convolution fusion | flops 1082392576 | bytes 5772800 | tf_op jit(solution)/shard_map/while/body/eval_jaxpr/dot_general | solution.py:33
  177.6 2.6 fusion.67
  180.1 2.2 exponential_reduce_fusion.2
  182.4 2.3 exponential_convert_fusion.2
  188.4 3.8 multiply_reduce_fusion.2
  192.2 5.6 %fusion.68 = bf16[1024,640]{1,0:T(8,128)(2,1)} fusion(bf16[1024,640]{1,0:T(8,128)(2,1)} %get-tuple-element.383, s32[]{:T(128)S(6)} %select_n.43, bf16[1024,2048]{1,0:T(8,128)(2,1)} %copy-done.1, bf16[1024,128]{1,0:T(8,128)(2,1)S(1)} %constant_dynamic-slice_fusion.2, f32[1024]{0:T(1024)S(1)} %get-tuple-element.364, ...), kind=kOutput, calls=%fused_computation.10.clone.1 | convolution fusion | flops 1082392576 | bytes 5772800 | tf_op jit(solution)/shard_map/while/body/eval_jaxpr/dot_general | solution.py:33
  198.2 2.6 fusion.67
  200.7 2.2 exponential_reduce_fusion.2
  203.0 2.3 exponential_convert_fusion.2
  209.0 3.8 multiply_reduce_fusion.2
  212.8 5.6 %fusion.68 = bf16[1024,640]{1,0:T(8,128)(2,1)} fusion(bf16[1024,640]{1,0:T(8,128)(2,1)} %get-tuple-element.383, s32[]{:T(128)S(6)} %select_n.43, bf16[1024,2048]{1,0:T(8,128)(2,1)} %copy-done.1, bf16[1024,128]{1,0:T(8,128)(2,1)S(1)} %constant_dynamic-slice_fusion.2, f32[1024]{0:T(1024)S(1)} %get-tuple-element.364, ...), kind=kOutput, calls=%fused_computation.10.clone.1 | convolution fusion | flops 1082392576 | bytes 5772800 | tf_op jit(solution)/shard_map/while/body/eval_jaxpr/dot_general | solution.py:33
  218.7 2.6 fusion.67
  221.3 2.2 exponential_reduce_fusion.2
  223.5 2.3 exponential_convert_fusion.2
  229.6 3.8 multiply_reduce_fusion.2
  233.4 5.6 %fusion.68 = bf16[1024,640]{1,0:T(8,128)(2,1)} fusion(bf16[1024,640]{1,0:T(8,128)(2,1)} %get-tuple-element.383, s32[]{:T(128)S(6)} %select_n.43, bf16[1024,2048]{1,0:T(8,128)(2,1)} %copy-done.1, bf16[1024,128]{1,0:T(8,128)(2,1)S(1)} %constant_dynamic-slice_fusion.2, f32[1024]{0:T(1024)S(1)} %get-tuple-element.364, ...), kind=kOutput, calls=%fused_computation.10.clone.1 | convolution fusion | flops 1082392576 | bytes 5772800 | tf_op jit(solution)/shard_map/while/body/eval_jaxpr/dot_general | solution.py:33
  239.3 2.4 collective-permute-start.1
  241.7 24.9 %all_to_all.134 = bf16[8,128,640]{2,1,0:T(8,128)(2,1)} all-to-all(bf16[8,128,640]{2,1,0:T(8,128)(2,1)} %bitcast.88), channel_id=1, replica_groups=mesh['blk'=32,'uly'=8] {'uly'}, dimensions={0} | all-to-all | bytes 2621440 | tf_op jit(solution)/shard_map/all_to_all | solution.py:93
  266.7 5.5 %all-to-all-start.4 = ((bf16[8,128,640]{2,1,0:T(8,128)(2,1)}), bf16[8,128,640]{2,1,0:T(8,128)(2,1)S(1)}, u32[]{:S(2)}, u32[]{:S(2)}) async-start(bf16[8,128,640]{2,1,0:T(8,128)(2,1)} %bitcast.87), calls=%async_computation.4 | async-start | bytes 2621440 | tf_op jit(solution)/shard_map/all_to_all | solution.py:92
  272.6 3.8 add_convert_fusion
  276.4 12.2 %all-to-all-done.4 = bf16[8,128,640]{2,1,0:T(8,128)(2,1)S(1)} async-done(((bf16[8,128,640]{2,1,0:T(8,128)(2,1)}), bf16[8,128,640]{2,1,0:T(8,128)(2,1)S(1)}, u32[]{:S(2)}, u32[]{:S(2)}) %all-to-all-start.4) | async-done | bytes 1310752 | tf_op jit(solution)/shard_map/all_to_all | solution.py:92
  288.7 7.9 %all-to-all-start.6 = ((bf16[8,128,640]{2,1,0:T(8,128)(2,1)}), bf16[8,128,640]{2,1,0:T(8,128)(2,1)}, u32[]{:S(2)}, u32[]{:S(2)}) async-start(bf16[8,128,640]{2,1,0:T(8,128)(2,1)} %bitcast.93), calls=%async_computation.6 | async-start | bytes 2621440 | tf_op jit(solution)/shard_map/all_to_all | solution.py:94
  296.6 1.8 copy.54
  298.3 1.6 fusion.27
  299.9 2.5 copy.53
  302.4 2.4 copy.56
  305.2 9.5 %all-to-all-done.6 = bf16[8,128,640]{2,1,0:T(8,128)(2,1)} async-done(((bf16[8,128,640]{2,1,0:T(8,128)(2,1)}), bf16[8,128,640]{2,1,0:T(8,128)(2,1)}, u32[]{:S(2)}, u32[]{:S(2)}) %all-to-all-start.6) | async-done | bytes 1310752 | tf_op jit(solution)/shard_map/all_to_all | solution.py:94
  314.7 1.8 copy.55
  316.9 1.6 fusion.28
  318.5 2.0 convolution_bitcast_fusion
  320.5 139.1 %all-reduce.2 = (bf16[5120,128]{0,1:T(8,128)(2,1)}, bf16[64,5120]{1,0:T(8,128)(2,1)S(1)}, bf16[64,5120]{1,0:T(8,128)(2,1)}) all-reduce(f32[5120,128]{0,1:T(8,128)} %convolution_bitcast_fusion, f32[64,5120]{1,0:T(8,128)S(1)} %copy-done.4, f32[64,5120]{1,0:T(8,128)} %fusion.28), channel_id=1, replica_groups=mesh['blk'=32,'uly'=8] {'blk','uly'}, use_global_device_ids=true, to_apply=%region_5.6 | all-reduce | flops 1310720 | bytes 7864320 | tf_op jit(solution)/shard_map/psum | solution.py:106
  459.6 2.4 fusion.25
  462.0 1.5 dynamic-slice_convert_fusion
  (80 shorter events, 24.7 us)
Async XLA Ops:
  0.6 1.3 copy-start
  0.6 3.0 copy-start.10
  6.5 24.9 %all-to-all-start.2 = ((bf16[128,8,640]{2,0,1:T(8,128)(2,1)}), bf16[128,8,640]{2,0,1:T(8,128)(2,1)S(1)}, u32[]{:S(2)}, u32[]{:S(2)}) async-start(bf16[128,8,640]{2,0,1:T(8,128)(2,1)} %bitcast.90), calls=%async_computation.2 | async-start | bytes 2621440 | tf_op jit(solution)/shard_map/all_to_all | solution.py:52
  53.9 1.9 copy-start.2
  55.8 60.1 %collective-permute-start = (bf16[2,1024,640]{2,1,0:T(8,128)(2,1)}, bf16[2,1024,640]{2,1,0:T(8,128)(2,1)}, u32[]{:S(2)}, u32[]{:S(2)}) collective-permute-start(bf16[2,1024,640]{2,1,0:T(8,128)(2,1)} %pad_maximum_fusion), channel_id=1, source_target_pairs={{0,8},{8,16},{16,24},{24,32},{32,40},{40,48},{48,56},{56,64},{64,7... | collective-permute-start | bytes 7864328 | tf_op jit(solution)/shard_map/ppermute | solution.py:12
  64.0 7.8 %copy-start.7 = (bf16[64,5120]{1,0:T(8,128)(2,1)S(1)}, bf16[64,5120]{1,0:T(8,128)(2,1)}, u32[]{:S(2)}) copy-start(bf16[64,5120]{1,0:T(8,128)(2,1)} %param.17) | copy-start | bytes 1966084
  64.0 43.7 %all-to-all-start.3 = ((bf16[128,8,640]{0,2,1:T(8,128)(2,1)}), bf16[128,8,640]{0,2,1:T(8,128)(2,1)}, u32[]{:S(2)}, u32[]{:S(2)}) async-start(bf16[128,8,640]{0,2,1:T(8,128)(2,1)} %bitcast.89), calls=%async_computation.3 | async-start | bytes 2621440 | tf_op jit(solution)/shard_map/all_to_all | solution.py:53
  70.0 1.8 copy-start.11
  107.7 24.0 %all-to-all-start = ((bf16[128,8,640]{2,0,1:T(8,128)(2,1)}), bf16[128,8,640]{2,0,1:T(8,128)(2,1)}, u32[]{:S(2)}, u32[]{:S(2)}) async-start(bf16[128,8,640]{2,0,1:T(8,128)(2,1)} %bitcast.86), calls=%async_computation | async-start | bytes 2621440 | tf_op jit(solution)/shard_map/all_to_all | solution.py:50
  116.0 2.1 copy-start.3
  143.4 2.5 copy-start.1
  164.0 2.5 copy-start.1
  184.6 2.5 copy-start.1
  205.2 2.5 copy-start.1
  225.8 2.5 copy-start.1
  239.3 27.4 %copy-start.6 = (bf16[1024,640]{1,0:T(8,128)(2,1)}, bf16[1024,640]{1,0:T(8,128)(2,1)S(1)}, u32[]{:S(2)}) copy-start(bf16[1024,640]{1,0:T(8,128)(2,1)S(1)} %get-tuple-element.177) | copy-start | bytes 3932164
  239.3 33.3 %collective-permute-start.1 = (f32[1024,640]{1,0:T(8,128)}, f32[1024,640]{1,0:T(8,128)}, u32[]{:S(2)}, u32[]{:S(2)}) collective-permute-start(f32[1024,640]{1,0:T(8,128)} %get-tuple-element.180), channel_id=1, source_target_pairs={{8,0},{16,8},{24,16},{32,24},{40,32},{48,40},{56,48},{64,56},{72,6... | collective-permute-start | bytes 7864328 | tf_op jit(solution)/shard_map/ppermute | solution.py:12
  266.7 22.0 %all-to-all-start.4 = ((bf16[8,128,640]{2,1,0:T(8,128)(2,1)}), bf16[8,128,640]{2,1,0:T(8,128)(2,1)S(1)}, u32[]{:S(2)}, u32[]{:S(2)}) async-start(bf16[8,128,640]{2,1,0:T(8,128)(2,1)} %bitcast.87), calls=%async_computation.4 | async-start | bytes 2621440 | tf_op jit(solution)/shard_map/all_to_all | solution.py:92
  288.7 7.9 %copy-start.5 = (bf16[8,128,640]{2,1,0:T(8,128)(2,1)}, bf16[8,128,640]{2,1,0:T(8,128)(2,1)S(1)}, u32[]{:S(2)}) copy-start(bf16[8,128,640]{2,1,0:T(8,128)(2,1)S(1)} %all-to-all-done.4) | copy-start | bytes 3932164
  288.7 26.1 %all-to-all-start.6 = ((bf16[8,128,640]{2,1,0:T(8,128)(2,1)}), bf16[8,128,640]{2,1,0:T(8,128)(2,1)}, u32[]{:S(2)}, u32[]{:S(2)}) async-start(bf16[8,128,640]{2,1,0:T(8,128)(2,1)} %bitcast.93), calls=%async_computation.6 | async-start | bytes 2621440 | tf_op jit(solution)/shard_map/all_to_all | solution.py:94
  299.9 4.9 %copy-start.8 = (bf16[64,5120]{1,0:T(8,128)(2,1)S(1)}, bf16[64,5120]{1,0:T(8,128)(2,1)}, u32[]{:S(2)}) copy-start(bf16[64,5120]{1,0:T(8,128)(2,1)} %param.17) | copy-start | bytes 1966084
  305.2 11.3 %copy-start.9 = (bf16[64,5120]{1,0:T(8,128)(2,1)S(1)}, bf16[64,5120]{1,0:T(8,128)(2,1)}, u32[]{:S(2)}) copy-start(bf16[64,5120]{1,0:T(8,128)(2,1)} %param.19) | copy-start | bytes 1966084
  318.5 2.0 copy-start.4
where the time goes:
time: 466 us; the launch traced here: 464 us
  blocking collectives  187 us (40%)
  waiting for transfers between devices  78.9 us (17%)
  matrix products  78.2 us (17%)
  local copies, waits for them, and re-layouts  44.3 us (10%)
  starting transfers between devices  40.1 us (9%)
  other arithmetic  34.9 us (7%)
    psum x1, blocking collectives, per_device(): lax.psum((down_terms, up_q_terms, up_v_terms), ('blk', 'uly'))  139 us
    all_to_all x1, waiting for transfers between devices, per_device(): lax.all_to_all(out_grad, 'uly', split_axis=1, concat_axis=0, tiled=True)  34.2 us
    dot_general x5, matrix products, head_pass(): jnp.dot(score_grad, keys, preferred_element_type=jnp.float32) * scale  28.2 us
    all_to_all x1, blocking collectives, per_device(): lax.all_to_all(query_grad_h, 'uly', split_axis=0, concat_axis=1, tiled=True)  24.9 us
    all_to_all x1, blocking collectives, per_device(): lax.all_to_all(key_base, 'uly', split_axis=1, concat_axis=0, tiled=True)  22.6 us
    dot_general x5, matrix products, head_pass(): jnp.dot(probs, values, preferred_element_type=jnp.float32)  19.2 us
    all_to_all x1, waiting for transfers between devices, per_device(): lax.all_to_all(value, 'uly', split_axis=1, concat_axis=0, tiled=True)  15.6 us
    dot_general x5, matrix products, head_pass(): scores = jnp.dot(query, keys.T, preferred_element_type=jnp.float32) * scale  12.8 us
  transfers between devices with their start and end apart: 7, of which 6 were waited for; matrix products, arithmetic and copies ran while one was open for 7% of the time, Pallas kernels for 0%

commit v1 on v0

--- a/solution.py
+++ b/solution.py
@@ -1,9 +1,20 @@
+import functools
 import jax
 import jax.numpy as jnp
 from jax import lax
 from jax.sharding import PartitionSpec as P
+from jax.lax import psum
 
 HEAD = 128
+
+
+def mark_grid_all(xin, a_name, ax_name):
+    for j0 in (a_name, ax_name):
+        xin = psum(xin, j0)
+    return xin
+
+
+follow_blocks = functools.partial(mark_grid_all, a_name="blk", ax_name="uly")
 
 
 def passed_along(block, axis, distance):
@@ -103,9 +114,7 @@
     down_terms = inner(tokens, lowrank)
     up_q_terms = inner(low_q, query_grad)
     up_v_terms = inner(low_v, value_grad)
-    down_total, up_q_total, up_v_total = lax.psum(
-        (down_terms, up_q_terms, up_v_terms), ("blk", "uly")
-    )
+    down_total, up_q_total, up_v_total = follow_blocks((down_terms, up_q_terms, up_v_terms))
     up_q_part = lax.dynamic_slice_in_dim(up_q_total, first_col, width, 1)
     up_v_part = lax.dynamic_slice_in_dim(up_v_total, first_col, width, 1)
     return (

time: 466 us -> 669 us (1.44)
  waiting for transfers between devices: 78.9 us -> 319 us
  blocking collectives: 187 us -> 130 us
  between operations: 0.8 us -> 14.2 us
    psum x0 -> x1, waiting for transfers between devices: none -> 218 us  [mark_grid_all(): xin = psum(xin, j0)]
    psum x1, blocking collectives: 139 us -> 107 us  [mark_grid_all(): xin = psum(xin, j0)]
    all_to_all x1 -> x0, blocking collectives: 24.9 us -> none  [per_device(): lax.all_to_all(query_grad_h, 'uly', split_axis=0, concat_axis=1, tiled=True)]
    ppermute x2, waiting for transfers between devices: 0.45 us -> 25 us  [passed_along(): return lax.ppermute(block, axis, route)]
  transfers between devices with their start and end apart: 7 -> 9, of which waited for: 6 -> 7; matrix products, arithmetic and copies ran while one was open for 7% -> 5% of each run, Pallas kernels for 0% -> 0%
where the time goes in v1:
time: 669 us; the launch traced here: 663 us
  waiting for transfers between devices  319 us (48%)
  blocking collectives  130 us (19%)
  matrix products  78.2 us (12%)
  starting transfers between devices  44.5 us (7%)
  local copies, waits for them, and re-layouts  42 us (6%)
  other arithmetic  35 us (5%)
  between operations  14.2 us (2%)
    psum x1, waiting for transfers between devices, mark_grid_all(): xin = psum(xin, j0)  218 us
    psum x1, blocking collectives, mark_grid_all(): xin = psum(xin, j0)  107 us
    all_to_all x1, waiting for transfers between devices, per_device(): lax.all_to_all(out_grad, 'uly', split_axis=1, concat_axis=0, tiled=True)  34.2 us
    dot_general x5, matrix products, head_pass(): jnp.dot(score_grad, keys, preferred_element_type=jnp.float32) * scale  28.2 us
    ppermute x2, waiting for transfers between devices, passed_along(): return lax.ppermute(block, axis, route)  25 us
    all_to_all x1, blocking collectives, per_device(): lax.all_to_all(key_base, 'uly', split_axis=1, concat_axis=0, tiled=True)  22.6 us
    dot_general x5, matrix products, head_pass(): jnp.dot(probs, values, preferred_element_type=jnp.float32)  19.2 us
    all_to_all x1, waiting for transfers between devices, per_device(): lax.all_to_all(value, 'uly', split_axis=1, concat_axis=0, tiled=True)  15.6 us
  transfers between devices with their start and end apart: 9, of which 7 were waited for; matrix products, arithmetic and copies ran while one was open for 5% of the time, Pallas kernels for 0%

profile of v1, /device:TPU:7, one launch (start us, length us, event | category | flops | bytes accessed | tf_op | source)
XLA Modules:
  0.0 663.3 jit_solution(13912225079041169830)
XLA Ops:
  7.2 1.3 copy-done
  8.5 1.7 convolution_convert_fusion.3
  10.2 1.6 fusion.20
  13.0 6.8 %all-to-all-start.2 = ((bf16[128,8,640]{2,0,1:T(8,128)(2,1)}), bf16[128,8,640]{2,0,1:T(8,128)(2,1)S(1)}, u32[]{:S(2)}, u32[]{:S(2)}) async-start(bf16[128,8,640]{2,0,1:T(8,128)(2,1)} %bitcast.90), calls=%async_computation.2 | async-start | bytes 2621440 | tf_op jit(solution)/shard_map/all_to_all | solution.py:63
  19.8 2.5 copy.67
  22.3 15.6 %all-to-all-done.2 = bf16[128,8,640]{2,0,1:T(8,128)(2,1)S(1)} async-done(((bf16[128,8,640]{2,0,1:T(8,128)(2,1)}), bf16[128,8,640]{2,0,1:T(8,128)(2,1)S(1)}, u32[]{:S(2)}, u32[]{:S(2)}) %all-to-all-start.2) | async-done | bytes 1310752 | tf_op jit(solution)/shard_map/all_to_all | solution.py:63
  37.9 22.6 %all_to_all.133 = bf16[128,8,640]{2,0,1:T(8,128)(2,1)S(1)} all-to-all(bf16[128,8,640]{2,0,1:T(8,128)(2,1)} %bitcast.91), channel_id=1, replica_groups=mesh['blk'=32,'uly'=8] {'uly'}, dimensions={1} | all-to-all | bytes 2621440 | tf_op jit(solution)/shard_map/all_to_all | solution.py:62
  60.5 1.9 pad_maximum_fusion
  62.4 5.6 collective-permute-start
  68.0 2.5 copy.48
  70.5 6.0 all-to-all-start.3
  76.5 1.8 convolution_convert_fusion.4
  80.0 34.2 %all-to-all-done.3 = bf16[128,8,640]{0,2,1:T(8,128)(2,1)} async-done(((bf16[128,8,640]{0,2,1:T(8,128)(2,1)}), bf16[128,8,640]{0,2,1:T(8,128)(2,1)}, u32[]{:S(2)}, u32[]{:S(2)}) %all-to-all-start.3) | async-done | bytes 1310752 | tf_op jit(solution)/shard_map/all_to_all | solution.py:64
  114.2 5.8 all-to-all-start
  120.0 2.4 copy.49
  122.5 2.0 slice_bitcast_fusion
  124.6 6.7 %pad_maximum_fusion.1 = (bf16[2048,640]{1,0:T(8,128)(2,1)}, bf16[2048,640]{1,0:T(8,128)(2,1)}) fusion(bf16[1024,640]{1,0:T(8,128)(2,1)S(1)} %bitcast.77, bf16[1024,640]{1,0:T(8,128)(2,1)S(1)} %get-tuple-element.292, bf16[1024,640]{1,0:T(8,128)(2,1)S(1)} %bitcast.75, bf16[1024,640]{1,0:T(8,128)(2,1)S(1)} %get-tuple-element.291), kind=kLoop, calls=%fused_computation.33 | loop fusion | flops 10485760 | bytes 10485760 | tf_op jit(solution)/shard_map/concatenate | solution.py:71
  131.3 6.9 %all-to-all-done = bf16[128,8,640]{2,0,1:T(8,128)(2,1)} async-done(((bf16[128,8,640]{2,0,1:T(8,128)(2,1)}), bf16[128,8,640]{2,0,1:T(8,128)(2,1)}, u32[]{:S(2)}, u32[]{:S(2)}) %all-to-all-start) | async-done | bytes 1310752 | tf_op jit(solution)/shard_map/all_to_all | solution.py:61
  138.2 1.6 broadcast_in_dim.43
  139.9 1.7 broadcast_in_dim.43.clone
  142.8 103.0 %while.20 = (s32[]{:T(128)}, bf16[1024,640]{1,0:T(8,128)(2,1)S(1)}, bf16[1024,640]{1,0:T(8,128)(2,1)}, f32[1024,640]{1,0:T(8,128)}, f32[1024,640]{1,0:T(8,128)},...) while((s32[]{:T(128)}, bf16[1024,640]{1,0:T(8,128)(2,1)S(1)}, ...), condition=%wide.region_4.5_spmd.clone, body=%wide.region_0.4_spmd.clone.sunk | while | flops 2718827520 | bytes 67680992 | solution.py:95
  142.8 2.6 fusion.67
  145.4 2.2 exponential_reduce_fusion.2
  147.6 2.3 exponential_convert_fusion.2
  153.7 3.8 multiply_reduce_fusion.2
  157.5 5.6 fusion.68
  163.4 2.6 fusion.67
  166.0 2.2 exponential_reduce_fusion.2
  168.2 2.3 exponential_convert_fusion.2
  174.2 3.8 multiply_reduce_fusion.2
  178.1 5.6 fusion.68
  184.0 2.6 fusion.67
  186.6 2.2 exponential_reduce_fusion.2
  188.8 2.3 exponential_convert_fusion.2
  194.8 3.8 multiply_reduce_fusion.2
  198.6 5.6 fusion.68
  204.6 2.6 fusion.67
  207.1 2.2 exponential_reduce_fusion.2
  209.4 2.3 exponential_convert_fusion.2
  215.5 3.8 multiply_reduce_fusion.2
  219.3 5.6 fusion.68
  225.2 2.6 fusion.67
  227.8 2.2 exponential_reduce_fusion.2
  230.0 2.3 exponential_convert_fusion.2
  236.1 3.8 multiply_reduce_fusion.2
  239.9 5.6 fusion.68
  245.8 2.4 collective-permute-start.1
  248.2 5.9 all-to-all-start.5
  254.2 25.0 %collective-permute-done.1 = f32[1024,640]{1,0:T(8,128)} collective-permute-done((f32[1024,640]{1,0:T(8,128)}, f32[1024,640]{1,0:T(8,128)}, u32[]{:S(2)}, u32[]{:S(2)}) %collective-permute-start.1) | collective-permute-done | bytes 2621472 | tf_op jit(solution)/shard_map/ppermute | solution.py:23
  279.1 3.9 add_convert_fusion
  283.0 6.4 all-to-all-start.6
  289.4 1.8 copy.54
  291.6 1.6 fusion.27
  293.2 7.5 %all-to-all-done.6 = bf16[8,128,640]{2,1,0:T(8,128)(2,1)} async-done(((bf16[8,128,640]{2,1,0:T(8,128)(2,1)}), bf16[8,128,640]{2,1,0:T(8,128)(2,1)}, u32[]{:S(2)}, u32[]{:S(2)}) %all-to-all-start.6) | async-done | bytes 1310752 | tf_op jit(solution)/shard_map/all_to_all | solution.py:105
  300.8 1.8 copy.55
  302.9 1.6 fusion.28
  304.5 2.0 convolution_bitcast_fusion
  306.6 5.6 all-to-all-start.4
  312.1 11.2 %all-to-all-done.4 = bf16[8,128,640]{2,1,0:T(8,128)(2,1)S(1)} async-done(((bf16[8,128,640]{2,1,0:T(8,128)(2,1)}), bf16[8,128,640]{2,1,0:T(8,128)(2,1)S(1)}, u32[]{:S(2)}, u32[]{:S(2)}) %all-to-all-start.4) | async-done | bytes 1310752 | tf_op jit(solution)/shard_map/all_to_all | solution.py:103
  323.3 1.5 copy.53
  324.8 2.4 copy.56
  327.3 218.5 %all-reduce.5.cloned.1.call-done = (f32[5120,128]{0,1:T(8,128)}, f32[64,5120]{1,0:T(8,128)}, f32[64,5120]{1,0:T(8,128)}) async-done(((f32[5120,128]{0,1:T(8,128)}, f32[64,5120]{1,0:T(8,128)}, f32[64,5120]{1,0:T(8,128)}), (f32[5120,128]{0,1:T(8,128)}, f32[64,5120]{1,0:T(8,128)}, f32[64,5120]{1,0:T(8,128)})) %all-reduce.5.cloned.1.call-update) | async-done | bytes 5242896 | tf_op jit(solution)/shard_map/psum | solution.py:13
  545.7 107.4 %all-reduce.6 = (bf16[5120,128]{0,1:T(8,128)(2,1)S(1)}, bf16[64,5120]{1,0:T(8,128)(2,1)S(1)}, bf16[64,5120]{1,0:T(8,128)(2,1)}) all-reduce(f32[5120,128]{0,1:T(8,128)} %get-tuple-element.279, f32[64,5120]{1,0:T(8,128)} %get-tuple-element.280, f32[64,5120]{1,0:T(8,128)} %get-tuple-element.281), channel_id=1, replica_groups=mesh['blk'=32,'uly'=8] {'uly'}, use_global_device_ids=true, to_apply=%region_6.7 | all-reduce | flops 1310720 | bytes 7864320 | tf_op jit(solution)/shard_map/psum | solution.py:13
  654.2 1.5 dynamic-slice_convert_fusion
  (82 shorter events, 26.7 us)
Async XLA Ops:
  7.2 1.3 copy-start
  7.2 3.0 copy-start.9
  13.0 24.9 %all-to-all-start.2 = ((bf16[128,8,640]{2,0,1:T(8,128)(2,1)}), bf16[128,8,640]{2,0,1:T(8,128)(2,1)S(1)}, u32[]{:S(2)}, u32[]{:S(2)}) async-start(bf16[128,8,640]{2,0,1:T(8,128)(2,1)} %bitcast.90), calls=%async_computation.2 | async-start | bytes 2621440 | tf_op jit(solution)/shard_map/all_to_all | solution.py:63
  60.5 1.9 copy-start.2
  62.4 60.1 %collective-permute-start = (bf16[2,1024,640]{2,1,0:T(8,128)(2,1)}, bf16[2,1024,640]{2,1,0:T(8,128)(2,1)}, u32[]{:S(2)}, u32[]{:S(2)}) collective-permute-start(bf16[2,1024,640]{2,1,0:T(8,128)(2,1)} %pad_maximum_fusion), channel_id=1, source_target_pairs={{0,8},{8,16},{16,24},{24,32},{32,40},{40,48},{48,56},{56,64},{64,7... | collective-permute-start | bytes 7864328 | tf_op jit(solution)/shard_map/ppermute | solution.py:23
  70.5 7.8 %copy-start.6 = (bf16[64,5120]{1,0:T(8,128)(2,1)S(1)}, bf16[64,5120]{1,0:T(8,128)(2,1)}, u32[]{:S(2)}) copy-start(bf16[64,5120]{1,0:T(8,128)(2,1)} %param.17) | copy-start | bytes 1966084
  70.5 43.7 %all-to-all-start.3 = ((bf16[128,8,640]{0,2,1:T(8,128)(2,1)}), bf16[128,8,640]{0,2,1:T(8,128)(2,1)}, u32[]{:S(2)}, u32[]{:S(2)}) async-start(bf16[128,8,640]{0,2,1:T(8,128)(2,1)} %bitcast.89), calls=%async_computation.3 | async-start | bytes 2621440 | tf_op jit(solution)/shard_map/all_to_all | solution.py:64
  76.5 1.8 copy-start.10
  114.2 24.0 %all-to-all-start = ((bf16[128,8,640]{2,0,1:T(8,128)(2,1)}), bf16[128,8,640]{2,0,1:T(8,128)(2,1)}, u32[]{:S(2)}, u32[]{:S(2)}) async-start(bf16[128,8,640]{2,0,1:T(8,128)(2,1)} %bitcast.85), calls=%async_computation | async-start | bytes 2621440 | tf_op jit(solution)/shard_map/all_to_all | solution.py:61
  122.5 2.1 copy-start.3
  149.9 2.5 copy-start.1
  170.5 2.5 copy-start.1
  191.1 2.5 copy-start.1
  211.6 2.5 copy-start.1
  232.3 2.5 copy-start.1
  245.8 2.4 copy-start.5
  245.8 33.3 %collective-permute-start.1 = (f32[1024,640]{1,0:T(8,128)}, f32[1024,640]{1,0:T(8,128)}, u32[]{:S(2)}, u32[]{:S(2)}) collective-permute-start(f32[1024,640]{1,0:T(8,128)} %get-tuple-element.180), channel_id=1, source_target_pairs={{8,0},{16,8},{24,16},{32,24},{40,32},{48,40},{56,48},{64,56},{72,6... | collective-permute-start | bytes 7864328 | tf_op jit(solution)/shard_map/ppermute | solution.py:23
  248.2 34.8 %all-to-all-start.5 = ((bf16[8,128,640]{2,1,0:T(8,128)(2,1)}), bf16[8,128,640]{2,1,0:T(8,128)(2,1)S(1)}, u32[]{:S(2)}, u32[]{:S(2)}) async-start(bf16[8,128,640]{2,1,0:T(8,128)(2,1)} %bitcast.88), calls=%async_computation.5 | async-start | bytes 2621440 | tf_op jit(solution)/shard_map/all_to_all | solution.py:104
  283.0 6.4 copy-start.4
  283.0 8.2 %copy-start.7 = (bf16[64,5120]{1,0:T(8,128)(2,1)S(1)}, bf16[64,5120]{1,0:T(8,128)(2,1)}, u32[]{:S(2)}) copy-start(bf16[64,5120]{1,0:T(8,128)(2,1)} %param.17) | copy-start | bytes 1966084
  283.0 17.7 %all-to-all-start.6 = ((bf16[8,128,640]{2,1,0:T(8,128)(2,1)}), bf16[8,128,640]{2,1,0:T(8,128)(2,1)}, u32[]{:S(2)}, u32[]{:S(2)}) async-start(bf16[8,128,640]{2,1,0:T(8,128)(2,1)} %bitcast.93), calls=%async_computation.6 | async-start | bytes 2621440 | tf_op jit(solution)/shard_map/all_to_all | solution.py:105
  289.4 256.3 %all-reduce.5.cloned.1.call-start = ((), (), s32[]{:S(2)}) async-start(), calls=%async_computation.7 | async-start | bytes 10485760 | tf_op jit(solution)/shard_map/psum | solution.py:13
  291.6 11.0 %copy-start.8 = (bf16[64,5120]{1,0:T(8,128)(2,1)S(1)}, bf16[64,5120]{1,0:T(8,128)(2,1)}, u32[]{:S(2)}) copy-start(bf16[64,5120]{1,0:T(8,128)(2,1)} %param.19) | copy-start | bytes 1966084
  306.6 16.8 %all-to-all-start.4 = ((bf16[8,128,640]{2,1,0:T(8,128)(2,1)}), bf16[8,128,640]{2,1,0:T(8,128)(2,1)S(1)}, u32[]{:S(2)}, u32[]{:S(2)}) async-start(bf16[8,128,640]{2,1,0:T(8,128)(2,1)} %bitcast.87), calls=%async_computation.4 | async-start | bytes 2621440 | tf_op jit(solution)/shard_map/all_to_all | solution.py:103
Sparse Core Ops, SparseCore 0:
  306.7 239.0 all-reduce.4
